TPU v7x, 256 devices: a whole 4x4x8 slice. The times are simulated.
256 devices in a mesh: seq: 64 (over x, z, core), head: 4 (over y).
Axes of the slice: x: 4, y: 4, z: 8, core: 2. Of those that a mesh axis runs over, the one named last changes fastest.
Arguments:
- tree_queries: bfloat16 [4, 64, 128, 128], P(None, 'seq', 'head'), may hold values from -100 to 100
- tree_keys: bfloat16 [4, 64, 8, 128], P(None, 'seq', 'head'), may hold values from -12 to 12
- tree_values: bfloat16 [4, 64, 8, 128], P(None, 'seq', 'head'), may hold values from -6 to 6
- cache_keys: bfloat16 [4, 40960, 8, 128], P(None, 'seq', 'head'), may hold values from -6 to 6
- cache_values: bfloat16 [4, 40960, 8, 128], P(None, 'seq', 'head'), may hold values from -6 to 6
- out_weight: bfloat16 [16384, 16384], P('head', 'seq'), may hold values from -0.8984375 to 0.8984375
- context_lengths: int32 [4], replicated, may hold values from 5120 to 40952, as said below
- parents: int32 [4, 64], replicated, may hold values from -1 to 62, as said below
- accepted_nodes: int32 [4, 8], replicated, may hold values from 0 to 63, as said below
- accepted_count: int32 [4], replicated, may hold values from 1 to 8
Outputs:
- projected: bfloat16 [256, 16384], P('head', 'seq')
- keys_out: bfloat16 [4, 40960, 8, 128], P(None, 'seq', 'head')
- values_out: bfloat16 [4, 40960, 8, 128], P(None, 'seq', 'head')
Inputs may be any that keep to these rules, and one draw needn't show every extreme that they name: Request r's cache holds positions 0 to context_lengths[r] - 1; some request has the largest value in every draw. parents[r, 0] = -1 marks the root; for i >= 1, 0 <= parents[r, i] < i. `accepted_nodes`: each row lists distinct tree nodes in increasing order, the first being the root 0; entries j >= accepted_count[r] are not used.
All inputs are finite; a program needn't handle non-finite values.
Results may differ from a plain program's by a relative error of at most 0.0051.
Values may be sent and summed in bfloat16 or wider, within the bound.
No kernel may reach another device: no remote copies, remote signals or barrier semaphores. Data moves between devices by JAX's collectives and lax.ppermute only.
A program may use at most 64 MiB of HBM per device.

v0:
```python
import math
import jax
import jax.numpy as jnp
from jax import lax
from jax.sharding import PartitionSpec as P

NEG = -1e30


def passed_along(block, axis, distance):
    devices = range(lax.axis_size(axis))
    route = [((i - distance) % len(devices), i) for i in devices]
    return lax.ppermute(block, axis, route)


def ancestors(parents):
    count_nodes = parents.shape[1]
    columns = jnp.arange(count_nodes, dtype=jnp.int32)
    linked = (parents[:, :, None] == columns[None, None, :]) | (
        columns[:, None] == columns[None, :]
    )[None]
    closure = linked.astype(jnp.float32)
    for rounds in range(max(count_nodes - 1, 1).bit_length()):
        closure = jnp.minimum(jnp.matmul(closure, closure, precision=lax.Precision.HIGHEST), 1.0)
    return closure


def partial_attention(queries, keys, values, allowed, scale_factor):
    scores = (
        jnp.einsum("rnhge,rphe->rnhgp", queries, keys, preferred_element_type=jnp.float32)
        * scale_factor
    )
    row_top = jnp.max(jnp.where(allowed, scores, NEG), axis=-1)
    weights = jnp.where(allowed, jnp.exp(scores - row_top[..., None]), 0.0)
    row_sum = jnp.sum(weights, axis=-1)
    numerator = jnp.einsum(
        "rnhgp,rphe->rnhge",
        weights.astype(jnp.bfloat16),
        values,
        preferred_element_type=jnp.float32,
    )
    return (row_top, row_sum, numerator)


def merge_parts(first, second):
    top_first, sum_first, acc_first = first
    top_second, sum_second, acc_second = second
    row_top = jnp.maximum(top_first, top_second)
    scale_first = jnp.exp(top_first - row_top)
    scale_second = jnp.exp(top_second - row_top)
    row_sum = sum_first * scale_first + sum_second * scale_second
    numerator = acc_first * scale_first[..., None] + acc_second * scale_second[..., None]
    return (row_top, row_sum, numerator)


def append_rows(cache_block, tree_all, choose, slot_map, written):
    picked = jnp.einsum(
        "rjn,rnhe->rjhe", choose, tree_all, preferred_element_type=jnp.float32
    ).astype(jnp.bfloat16)
    placed = jnp.einsum(
        "rjp,rjhe->rphe", slot_map, picked, preferred_element_type=jnp.float32
    ).astype(jnp.bfloat16)
    return jnp.where(written[:, :, None, None], placed, cache_block)


def on_device(
    tree_queries,
    tree_keys,
    tree_values,
    cache_keys,
    cache_values,
    out_weight,
    context_lengths,
    parents,
    accepted_nodes,
    accepted_count,
):
    requests, ctx_local, kv_local, head_dim = cache_keys.shape
    node_local, q_local = (tree_queries.shape[1], tree_queries.shape[2])
    group_size = q_local // kv_local
    path_len = accepted_nodes.shape[1]
    scale_factor = 1.0 / math.sqrt(head_dim)
    seq_index = lax.axis_index("seq")
    seq_count = lax.axis_size("seq")
    nodes_all = node_local * seq_count
    offset = seq_index * ctx_local
    grouped = tree_queries.reshape(requests, node_local, kv_local, group_size, head_dim)
    tree_all_k, tree_all_v = (
        lax.all_gather(tree_keys, "seq", axis=1, tiled=True),
        lax.all_gather(tree_values, "seq", axis=1, tiled=True),
    )
    closure = ancestors(parents)
    home_rows = lax.dynamic_slice_in_dim(closure, seq_index * node_local, node_local, 1)
    tree_state = partial_attention(
        grouped, tree_all_k, tree_all_v, home_rows[:, :, None, None, :] > 0.5, scale_factor
    )
    positions = offset + jnp.arange(ctx_local, dtype=jnp.int32)
    usable = (positions[None, :] < context_lengths[:, None])[:, None, None, None, :]

    def turn(turn_number, carried):
        queries, row_top, row_sum, numerator = carried
        local_part = partial_attention(queries, cache_keys, cache_values, usable, scale_factor)
        row_top, row_sum, numerator = merge_parts((row_top, row_sum, numerator), local_part)
        queries = passed_along(queries, "seq", 1)
        row_top, row_sum, numerator = passed_along((row_top, row_sum, numerator), "seq", 1)
        return (queries, row_top, row_sum, numerator)

    start_top = jnp.full((requests, node_local, kv_local, group_size), NEG, jnp.float32)
    start_sum = jnp.zeros((requests, node_local, kv_local, group_size), jnp.float32)
    start_acc = jnp.zeros((requests, node_local, kv_local, group_size, head_dim), jnp.float32)
    finished = lax.fori_loop(0, seq_count, turn, (grouped, start_top, start_sum, start_acc))
    cache_state = (finished[1], finished[2], finished[3])
    final_top, final_sum, final_acc = merge_parts(cache_state, tree_state)
    attention = (
        (final_acc / final_sum[..., None])
        .astype(jnp.bfloat16)
        .reshape(requests, node_local, q_local * head_dim)
    )
    partial_terms = jnp.einsum(
        "rnx,xd->rnd",
        lax.all_gather(attention, "seq", axis=1, tiled=True),
        out_weight,
        preferred_element_type=jnp.float32,
    )
    partial_terms = partial_terms.reshape(requests * nodes_all, out_weight.shape[1])
    projected = lax.psum_scatter(partial_terms, "head", scatter_dimension=0, tiled=True).astype(
        jnp.bfloat16
    )
    choose = (
        accepted_nodes[:, :, None] == jnp.arange(nodes_all, dtype=jnp.int32)[None, None, :]
    ).astype(jnp.bfloat16)
    steps_index = jnp.arange(path_len, dtype=jnp.int32)
    targets = context_lengths[:, None] + steps_index[None, :] - offset
    alive = steps_index[None, :] < accepted_count[:, None]
    slot_flags = (
        targets[:, :, None] == jnp.arange(ctx_local, dtype=jnp.int32)[None, None, :]
    ) & alive[:, :, None]
    slot_map = slot_flags.astype(jnp.bfloat16)
    written = jnp.sum(slot_flags.astype(jnp.float32), axis=1) > 0.5
    keys_out = append_rows(cache_keys, tree_all_k, choose, slot_map, written)
    values_out = append_rows(cache_values, tree_all_v, choose, slot_map, written)
    return (projected, keys_out, values_out)


def solution(mesh):
    in_specs = (
        P(None, "seq", "head", None),
        P(None, "seq", "head", None),
        P(None, "seq", "head", None),
        P(None, "seq", "head", None),
        P(None, "seq", "head", None),
        P("head", "seq"),
        P(),
        P(),
        P(),
        P(),
    )
    out_specs = (P("head", "seq"), P(None, "seq", "head", None), P(None, "seq", "head", None))
    return jax.shard_map(
        on_device, mesh=mesh, in_specs=in_specs, out_specs=out_specs, check_vma=False
    )
```

profile of v0, /device:TPU:2, one launch (start us, length us, event | category | flops | bytes accessed | tf_op | source)
XLA Modules:
  0.0 925.1 jit_solution(13085080901726072045)
XLA Ops:
  10.5 56.6 %all_gather.9 = bf16[4,64,2,128]{3,0,2,1:T(4,128)(2,1)} all-gather(bf16[4,1,2,128]{3,0,2,1:T(4,128)(2,1)S(1)} %copy.33), channel_id=1, replica_groups=mesh['seq'=64,'head'=4] {'seq'}, dimensions={1}, use_global_device_ids=true | all-gather | bytes 133120 | tf_op jit(solution)/shard_map/all_gather | solution.py:89
  70.1 51.7 %all_gather.10 = bf16[4,64,2,128]{3,0,2,1:T(4,128)(2,1)} all-gather(bf16[4,1,2,128]{3,0,2,1:T(4,128)(2,1)S(1)} %copy.35), channel_id=1, replica_groups=mesh['seq'=64,'head'=4] {'seq'}, dimensions={1}, use_global_device_ids=true | all-gather | bytes 133120 | tf_op jit(solution)/shard_map/all_gather | solution.py:90
  122.9 645.8 %while.17 = (s32[]{:T(128)}, bf16[4,1,2,16,128]{4,3,2,0,1:T(8,128)(2,1)S(1)}, f32[4,1,2,16]{3,2,0,1:T(2,128)S(1)}, f32[4,1,2,16]{3,2,0,1:T(2,128)S(1)}, f32[4,1,...) while((s32[]{:T(128)}, ...), condition=%wide.region_3.4_spmd.clone, body=%wide.region_0.3_spmd.clone.sunk | while | flops 42732544 | bytes 9494321 | solution.py:111
  128.3 4.2 collective-permute-done.1
  136.4 5.9 collective-permute-done.1
  145.6 6.3 collective-permute-done.1
  155.2 6.3 collective-permute-done.1
  164.9 6.3 collective-permute-done.1
  174.5 6.3 collective-permute-done.1
  184.1 6.3 collective-permute-done.1
  193.7 6.3 collective-permute-done.1
  203.3 6.3 collective-permute-done.1
  213.0 6.3 collective-permute-done.1
  222.6 6.3 collective-permute-done.1
  232.2 6.3 collective-permute-done.1
  241.8 6.3 collective-permute-done.1
  251.5 6.3 collective-permute-done.1
  261.1 6.3 collective-permute-done.1
  270.7 6.3 collective-permute-done.1
  280.3 6.3 collective-permute-done.1
  289.9 6.3 collective-permute-done.1
  299.6 6.3 collective-permute-done.1
  309.2 6.3 collective-permute-done.1
  318.8 6.3 collective-permute-done.1
  328.4 6.3 collective-permute-done.1
  338.0 6.3 collective-permute-done.1
  347.7 6.3 collective-permute-done.1
  357.3 6.3 collective-permute-done.1
  366.9 6.3 collective-permute-done.1
  376.5 6.3 collective-permute-done.1
  386.2 6.3 collective-permute-done.1
  395.8 6.3 collective-permute-done.1
  405.4 6.3 collective-permute-done.1
  415.0 6.3 collective-permute-done.1
  424.6 6.3 collective-permute-done.1
  434.3 6.3 collective-permute-done.1
  443.9 6.3 collective-permute-done.1
  453.5 6.3 collective-permute-done.1
  464.2 5.2 collective-permute-done.1
  475.0 4.0 collective-permute-done.1
  492.8 3.9 collective-permute-start.2
  503.6 3.9 collective-permute-start.2
  514.4 3.9 collective-permute-start.2
  525.3 3.9 collective-permute-start.2
  536.1 3.9 collective-permute-start.2
  546.9 3.9 collective-permute-start.2
  557.8 3.9 collective-permute-start.2
  568.6 3.9 collective-permute-start.2
  579.4 3.9 collective-permute-start.2
  590.3 3.9 collective-permute-start.2
  601.1 3.9 collective-permute-start.2
  611.9 3.9 collective-permute-start.2
  622.8 3.9 collective-permute-start.2
  633.6 3.9 collective-permute-start.2
  644.4 3.9 collective-permute-start.2
  655.3 3.9 collective-permute-start.2
  666.1 3.9 collective-permute-start.2
  687.8 3.9 collective-permute-start.2
  720.2 3.9 collective-permute-start.2
  731.1 3.9 collective-permute-start.2
  763.6 3.9 collective-permute-start.2
  771.1 118.9 %all-gather.2.cloned.1.call-done = bf16[4,64,4096]{2,0,1:T(4,128)(2,1)} async-done(((bf16[4,1,4096]{2,0,1:T(4,128)(2,1)}), bf16[4,64,4096]{2,0,1:T(4,128)(2,1)}) %all-gather.2.cloned.1.call-update) | async-done | bytes 2097168 | tf_op jit(solution)/shard_map/all_gather | solution.py:121
  890.0 4.7 fusion.17
  906.2 10.7 %reduce-scatter.2.cloned.1.call-done = f32[64,256]{1,0:T(8,128)} async-done(((f32[256,256]{1,0:T(8,128)}), f32[64,256]{1,0:T(8,128)}) %reduce-scatter.2.cloned.1.call-update) | async-done | bytes 65552 | tf_op jit(solution)/shard_map/reduce_scatter | solution.py:126
  (1028 shorter events, 356.2 us)
Async XLA Ops:
  7.2 882.8 %all-gather.2.cloned.1.call-start = ((), (), s32[]{:S(2)}) async-start(), calls=%async_computation.1 | async-start | bytes 2129920 | tf_op jit(solution)/shard_map/all_gather | solution.py:121
  126.1 6.6 collective-permute-start.3
  135.9 6.5 collective-permute-start.3
  145.5 6.5 collective-permute-start.3
  155.1 6.5 collective-permute-start.3
  164.7 6.5 collective-permute-start.3
  174.4 6.5 collective-permute-start.3
  184.0 6.5 collective-permute-start.3
  232.1 6.5 collective-permute-start.3
  241.7 6.5 collective-permute-start.3
  251.3 6.5 collective-permute-start.3
  261.0 6.5 collective-permute-start.3
  270.6 6.5 collective-permute-start.3
  501.5 7.3 collective-permute-start.3
  501.5 7.2 collective-permute-start
  511.9 7.7 collective-permute-start.3
  511.9 7.7 collective-permute-start
  522.8 7.7 collective-permute-start.3
  522.8 7.7 collective-permute-start
  533.6 7.7 collective-permute-start.3
  533.6 7.7 collective-permute-start
  544.4 7.7 collective-permute-start.3
  544.4 7.7 collective-permute-start
  555.2 7.7 collective-permute-start.3
  555.3 7.7 collective-permute-start
  566.1 7.7 collective-permute-start.3
  566.1 7.7 collective-permute-start
  576.9 7.7 collective-permute-start.3
  576.9 7.7 collective-permute-start
  587.7 7.7 collective-permute-start.3
  587.7 7.7 collective-permute-start
  598.6 7.7 collective-permute-start.3
  598.6 7.7 collective-permute-start
  609.4 7.7 collective-permute-start.3
  609.4 7.7 collective-permute-start
  620.2 7.7 collective-permute-start.3
  620.2 7.7 collective-permute-start
  631.1 7.7 collective-permute-start.3
  631.1 7.7 collective-permute-start
  641.9 7.7 collective-permute-start.3
  641.9 7.7 collective-permute-start
  652.7 7.7 collective-permute-start.3
  652.7 7.7 collective-permute-start
  663.6 7.7 collective-permute-start.3
  663.6 7.7 collective-permute-start
  674.4 7.7 collective-permute-start.3
  674.4 7.7 collective-permute-start
  685.2 7.7 collective-permute-start.3
  685.2 7.7 collective-permute-start
  696.1 7.7 collective-permute-start.3
  696.1 7.7 collective-permute-start
  706.9 7.7 collective-permute-start.3
  706.9 7.7 collective-permute-start
  717.7 7.7 collective-permute-start.3
  717.7 7.7 collective-permute-start
  728.6 7.7 collective-permute-start.3
  728.6 7.7 collective-permute-start
  739.4 7.7 collective-permute-start.3
  739.4 7.7 collective-permute-start
  750.2 7.7 collective-permute-start.3
  750.2 7.7 collective-permute-start
  761.1 7.7 collective-permute-start.3
  761.1 7.7 collective-permute-start
  770.6 146.3 %reduce-scatter.2.cloned.1.call-start = ((), (), s32[]{:S(2)}) async-start(), calls=%async_computation.2 | async-start | bytes 327680 | tf_op jit(solution)/shard_map/reduce_scatter | solution.py:126
  (271 other events, 3287.4 us)
Sparse Core Ops, SparseCore 0:
  770.7 119.2 all-gather.1
  894.9 21.9 reduce-scatter.1
where the time goes:
time: 931 us; the launch traced here: 925 us
  waiting for transfers between devices  393 us (42%)
  starting transfers between devices  179 us (19%)
  matrix products  169 us (18%)
  blocking collectives  108 us (12%)
  local copies, waits for them, and re-layouts  36.9 us (4%)
  other arithmetic  22.3 us (2%)
  between operations  14.3 us (2%)
    ppermute x256, waiting for transfers between devices, passed_along(): return lax.ppermute(block, axis, route)  264 us
    ppermute x256, starting transfers between devices, passed_along(): return lax.ppermute(block, axis, route)  179 us
    dot_general x65, matrix products, partial_attention(): jnp.einsum('rnhgp,rphe->rnhge', weights.astype(jnp.bfloat16), values, pre...  119 us
    all_gather x1, waiting for transfers between devices, on_device(): lax.all_gather(attention, 'seq', axis=1, tiled=True)  119 us
    all_gather x1, blocking collectives, on_device(): lax.all_gather(tree_keys, 'seq', axis=1, tiled=True)  56.6 us
    all_gather x1, blocking collectives, on_device(): lax.all_gather(tree_values, 'seq', axis=1, tiled=True)  51.7 us
    dot_general x65, matrix products, partial_attention(): jnp.einsum('rnhge,rphe->rnhgp', queries, keys, preferred_element_type=jnp...  38.7 us
    while x192, local copies, waits for them, and re-layouts  24.2 us
  transfers between devices with their start and end apart: 258, of which 92 were waited for; matrix products, arithmetic and copies ran while one was open for 1% of the time, Pallas kernels for 0%

commit v1 on v0

--- a/solution.py
+++ b/solution.py
@@ -118,7 +118,9 @@
     )
     partial_terms = jnp.einsum(
         "rnx,xd->rnd",
-        lax.all_gather(attention, "seq", axis=1, tiled=True),
+        jnp.concatenate(
+            lax.all_to_all(jnp.stack([attention] * lax.axis_size("seq")), "seq", 0, 0), axis=1
+        ),
         out_weight,
         preferred_element_type=jnp.float32,
     )

time: 931 us -> 917 us (0.985)
  waiting for transfers between devices: 393 us -> 321 us
  starting transfers between devices: 179 us -> 236 us
    all_gather x1 -> x0, waiting for transfers between devices: 119 us -> none  [on_device(): lax.all_gather(attention, 'seq', axis=1, tiled=True)]
    all_to_all x0 -> x1, starting transfers between devices: none -> 54.4 us  [on_device(): lax.all_to_all(jnp.stack([attention] * lax.axis_size('seq')), 'seq', 0, 0)]
    all_to_all x0 -> x1, waiting for transfers between devices: none -> 48.7 us  [on_device(): lax.all_to_all(jnp.stack([attention] * lax.axis_size('seq')), 'seq', 0, 0)]
  transfers between devices with their start and end apart: 258 -> 258, of which waited for: 92 -> 93; matrix products, arithmetic and copies ran while one was open for 1% -> 1% of each run, Pallas kernels for 0% -> 0%
where the time goes in v1:
time: 917 us; the launch traced here: 911 us
  waiting for transfers between devices  321 us (35%)
  starting transfers between devices  236 us (26%)
  matrix products  166 us (18%)
  blocking collectives  108 us (12%)
  local copies, waits for them, and re-layouts  41.4 us (5%)
  other arithmetic  22.3 us (2%)
  between operations  14.3 us (2%)
    ppermute x256, waiting for transfers between devices, passed_along(): return lax.ppermute(block, axis, route)  261 us
    ppermute x256, starting transfers between devices, passed_along(): return lax.ppermute(block, axis, route)  181 us
    dot_general x65, matrix products, partial_attention(): jnp.einsum('rnhgp,rphe->rnhge', weights.astype(jnp.bfloat16), values, pre...  120 us
    all_gather x1, blocking collectives, on_device(): lax.all_gather(tree_keys, 'seq', axis=1, tiled=True)  56.3 us
    all_to_all x1, starting transfers between devices, on_device(): lax.all_to_all(jnp.stack([attention] * lax.axis_size('seq')), 'seq', 0, 0)  54.4 us
    all_gather x1, blocking collectives, on_device(): lax.all_gather(tree_values, 'seq', axis=1, tiled=True)  51.8 us
    all_to_all x1, waiting for transfers between devices, on_device(): lax.all_to_all(jnp.stack([attention] * lax.axis_size('seq')), 'seq', 0, 0)  48.7 us
    dot_general x65, matrix products, partial_attention(): jnp.einsum('rnhge,rphe->rnhgp', queries, keys, preferred_element_type=jnp...  38.7 us
  transfers between devices with their start and end apart: 258, of which 93 were waited for; matrix products, arithmetic and copies ran while one was open for 1% of the time, Pallas kernels for 0%

profile of v1, /device:TPU:2, one launch (start us, length us, event | category | flops | bytes accessed | tf_op | source)
XLA Modules:
  0.0 911.3 jit_solution(13071482364089437763)
XLA Ops:
  10.5 56.3 %all_gather.6 = bf16[4,64,2,128]{3,0,2,1:T(4,128)(2,1)} all-gather(bf16[4,1,2,128]{3,0,2,1:T(4,128)(2,1)S(1)} %copy.31), channel_id=1, replica_groups=mesh['seq'=64,'head'=4] {'seq'}, dimensions={1}, use_global_device_ids=true | all-gather | bytes 133120 | tf_op jit(solution)/shard_map/all_gather | solution.py:89
  69.8 51.8 %all_gather.7 = bf16[4,64,2,128]{3,0,2,1:T(4,128)(2,1)} all-gather(bf16[4,1,2,128]{3,0,2,1:T(4,128)(2,1)S(1)} %copy.33), channel_id=1, replica_groups=mesh['seq'=64,'head'=4] {'seq'}, dimensions={1}, use_global_device_ids=true | all-gather | bytes 133120 | tf_op jit(solution)/shard_map/all_gather | solution.py:90
  122.7 646.6 %while.17 = (s32[]{:T(128)}, bf16[4,1,2,16,128]{4,3,2,0,1:T(8,128)(2,1)S(1)}, f32[4,1,2,16]{3,2,0,1:T(2,128)S(1)}, f32[4,1,2,16]{3,2,0,1:T(2,128)S(1)}, f32[4,1,...) while((s32[]{:T(128)}, ...), condition=%wide.region_3.4_spmd.clone, body=%wide.region_0.3_spmd.clone.sunk | while | flops 42732544 | bytes 9494321 | solution.py:111
  128.3 4.0 collective-permute-done.1
  136.0 6.0 collective-permute-done.1
  145.3 6.3 collective-permute-done.1
  154.9 6.3 collective-permute-done.1
  164.6 6.3 collective-permute-done.1
  174.2 6.3 collective-permute-done.1
  183.8 6.3 collective-permute-done.1
  193.4 6.3 collective-permute-done.1
  203.1 6.3 collective-permute-done.1
  212.7 6.3 collective-permute-done.1
  222.3 6.3 collective-permute-done.1
  232.0 6.3 collective-permute-done.1
  241.6 6.3 collective-permute-done.1
  251.2 6.3 collective-permute-done.1
  260.8 6.3 collective-permute-done.1
  270.5 6.3 collective-permute-done.1
  280.1 6.3 collective-permute-done.1
  289.7 6.3 collective-permute-done.1
  299.4 6.3 collective-permute-done.1
  309.0 6.3 collective-permute-done.1
  318.6 6.3 collective-permute-done.1
  328.2 6.3 collective-permute-done.1
  337.9 6.3 collective-permute-done.1
  347.5 6.3 collective-permute-done.1
  357.1 6.3 collective-permute-done.1
  366.8 6.3 collective-permute-done.1
  376.4 6.3 collective-permute-done.1
  386.0 6.3 collective-permute-done.1
  395.6 6.3 collective-permute-done.1
  405.3 6.3 collective-permute-done.1
  414.9 6.3 collective-permute-done.1
  424.5 6.3 collective-permute-done.1
  434.2 6.3 collective-permute-done.1
  443.8 6.3 collective-permute-done.1
  453.7 6.0 collective-permute-done.1
  464.6 4.8 collective-permute-done.1
  482.3 3.9 collective-permute-start.2
  493.2 3.9 collective-permute-start.2
  504.0 3.9 collective-permute-start.2
  514.8 3.9 collective-permute-start.2
  525.7 3.9 collective-permute-start.2
  536.5 3.9 collective-permute-start.2
  547.4 3.9 collective-permute-start.2
  558.2 3.9 collective-permute-start.2
  569.0 3.9 collective-permute-start.2
  579.9 3.9 collective-permute-start.2
  590.7 3.9 collective-permute-start.2
  601.6 3.9 collective-permute-start.2
  612.4 3.9 collective-permute-start.2
  623.2 3.9 collective-permute-start.2
  634.1 3.9 collective-permute-start.2
  644.9 3.9 collective-permute-start.2
  655.7 3.9 collective-permute-start.2
  666.6 3.9 collective-permute-start.2
  677.4 3.9 collective-permute-start.2
  688.3 3.9 collective-permute-start.2
  720.8 3.9 collective-permute-start.2
  753.3 3.9 collective-permute-start.2
  772.8 54.4 %all-to-all-start = ((bf16[64,4,1,4096]{3,1,2,0:T(4,128)(2,1)}), bf16[64,4,1,4096]{3,1,2,0:T(4,128)(2,1)}, u32[]{:S(2)}, u32[]{:S(2)}) async-start(bf16[64,4,1,4096]{3,1,2,0:T(4,128)(2,1)} %stack.3), calls=%async_computation | async-start | bytes 4194304 | tf_op jit(solution)/shard_map/all_to_all | solution.py:122
  827.8 48.7 %all-to-all-done = bf16[64,4,1,4096]{3,1,2,0:T(4,128)(2,1)} async-done(((bf16[64,4,1,4096]{3,1,2,0:T(4,128)(2,1)}), bf16[64,4,1,4096]{3,1,2,0:T(4,128)(2,1)}, u32[]{:S(2)}, u32[]{:S(2)}) %all-to-all-start) | async-done | bytes 2097184 | tf_op jit(solution)/shard_map/all_to_all | solution.py:122
  892.2 10.8 %reduce-scatter.2.cloned.1.call-done = f32[64,256]{1,0:T(8,128)} async-done(((f32[256,256]{1,0:T(8,128)}), f32[64,256]{1,0:T(8,128)}) %reduce-scatter.2.cloned.1.call-update) | async-done | bytes 65552 | tf_op jit(solution)/shard_map/reduce_scatter | solution.py:128
  (1029 shorter events, 363.8 us)
Async XLA Ops:
  125.9 6.5 collective-permute-start.3
  135.6 6.5 collective-permute-start.3
  145.2 6.5 collective-permute-start.3
  154.8 6.5 collective-permute-start.3
  164.4 6.5 collective-permute-start.3
  174.1 6.5 collective-permute-start.3
  183.7 6.5 collective-permute-start.3
  193.3 6.5 collective-permute-start.3
  212.6 6.5 collective-permute-start.3
  222.2 6.5 collective-permute-start.3
  491.8 6.5 collective-permute-start.3
  491.8 6.5 collective-permute-start
  501.5 7.7 collective-permute-start.3
  501.5 7.7 collective-permute-start
  512.3 7.7 collective-permute-start.3
  512.3 7.7 collective-permute-start
  523.2 7.7 collective-permute-start.3
  523.2 7.7 collective-permute-start
  534.0 7.7 collective-permute-start.3
  534.0 7.7 collective-permute-start
  544.8 7.7 collective-permute-start.3
  544.8 7.7 collective-permute-start
  555.7 7.7 collective-permute-start.3
  555.7 7.7 collective-permute-start
  566.5 7.7 collective-permute-start.3
  566.5 7.7 collective-permute-start
  577.4 7.7 collective-permute-start.3
  577.4 7.7 collective-permute-start
  588.2 7.7 collective-permute-start.3
  588.2 7.7 collective-permute-start
  599.0 7.7 collective-permute-start.3
  599.0 7.7 collective-permute-start
  609.9 7.7 collective-permute-start.3
  609.9 7.7 collective-permute-start
  620.7 7.7 collective-permute-start.3
  620.7 7.7 collective-permute-start
  631.6 7.7 collective-permute-start.3
  631.6 7.7 collective-permute-start
  642.4 7.7 collective-permute-start.3
  642.4 7.7 collective-permute-start
  653.2 7.7 collective-permute-start.3
  653.2 7.7 collective-permute-start
  664.1 7.7 collective-permute-start.3
  664.1 7.7 collective-permute-start
  674.9 7.7 collective-permute-start.3
  674.9 7.7 collective-permute-start
  685.7 7.7 collective-permute-start.3
  685.8 7.7 collective-permute-start
  696.6 7.7 collective-permute-start.3
  696.6 7.7 collective-permute-start
  707.4 7.7 collective-permute-start.3
  707.4 7.7 collective-permute-start
  718.3 7.7 collective-permute-start.3
  718.3 7.7 collective-permute-start
  729.1 7.7 collective-permute-start.3
  729.1 7.7 collective-permute-start
  739.9 7.7 collective-permute-start.3
  739.9 7.7 collective-permute-start
  750.8 7.7 collective-permute-start.3
  750.8 7.7 collective-permute-start
  761.6 7.7 collective-permute-start.3
  761.6 7.7 collective-permute-start
  772.8 103.7 %all-to-all-start = ((bf16[64,4,1,4096]{3,1,2,0:T(4,128)(2,1)}), bf16[64,4,1,4096]{3,1,2,0:T(4,128)(2,1)}, u32[]{:S(2)}, u32[]{:S(2)}) async-start(bf16[64,4,1,4096]{3,1,2,0:T(4,128)(2,1)} %stack.3), calls=%async_computation | async-start | bytes 4194304 | tf_op jit(solution)/shard_map/all_to_all | solution.py:122
  827.3 75.7 %reduce-scatter.2.cloned.1.call-start = ((), (), s32[]{:S(2)}) async-start(), calls=%async_computation.2 | async-start | bytes 327680 | tf_op jit(solution)/shard_map/reduce_scatter | solution.py:128
  (271 other events, 2316.2 us)
Sparse Core Ops, SparseCore 0:
  880.9 22.0 reduce-scatter.1
